TPU v7x, 128 devices: a whole 4x4x4 slice. The times are simulated.
128 devices in a mesh: pix: 64 (over x, z, y_hi, core), col: 2 (over y_lo).
Axes of the slice: x: 4, y: 4 (y_hi: 2, y_lo: 2; y = y_hi * 2 + y_lo), z: 4, core: 2. Of those that a mesh axis runs over, the one named last changes fastest.
Arguments:
- observed: float32 [16384, 4096], P('pix', 'col'), may hold values from -40 to 40
- valid_mask: int32 [16384, 512], P('pix', 'col'), may hold values 0 or 1
- pix_factor: float32 [16384, 256], P('pix'), may hold values from -6 to 6
- col_factor: float32 [4096, 256], P('col'), may hold values from -0.375 to 0.375
Outputs:
- pix_next: float32 [16384, 256], P('pix')
- col_next: float32 [4096, 256], P('col')
- cloud: float32 [16384, 4096], P('pix', 'col')
All inputs are finite; a program needn't handle non-finite values. No bound on the sum of `valid_mask` on one device may be relied on, other than what follows from the above.
Results may differ from a plain program's by a relative error of at most 0.0003.
Values sent between devices are 32-bit elements; how exact they have to be, the bound alone decides.
A program may use at most 64 MiB of HBM per device.

v0:
```python
import jax
import jax.numpy as jnp
from jax import lax
from jax.sharding import PartitionSpec as P

BANDS = 8
WIDTH = 256
ITERS = 2
PASSES = 2
highest = lax.Precision.HIGHEST
threshold_scale = 1.0
diffusion = 0.2


def passed_along(block, axis, distance):
    devices = range(lax.axis_size(axis))
    route = [(i - distance, i) for i in devices if i - distance in devices]
    return lax.ppermute(block, axis, route)


def soft_cut(values, level):
    return jnp.sign(values) * jnp.maximum(jnp.abs(values) - level, 0.0)


def flux_of(diff, level):
    return diff / (1.0 + (diff / level) ** 2)


def level_of(residual, weight, total):
    spread = lax.psum(jnp.sum(weight * residual * residual), ("pix", "col"))
    return threshold_scale * jnp.sqrt(spread / total + 1e-06)


def smooth_pass(grid, level, strip_index, pix_count):
    has_north = strip_index > 0
    has_south = strip_index < pix_count - 1
    top_row = grid[0]
    bottom_row = grid[-1]
    north_rim = passed_along(bottom_row, "pix", 1)
    south_rim = passed_along(top_row, "pix", -1)
    north_rim = jnp.where(has_north, north_rim, top_row)
    south_rim = jnp.where(has_south, south_rim, bottom_row)
    north = jnp.concatenate([north_rim[None], grid[:-1]], axis=0)
    south = jnp.concatenate([grid[1:], south_rim[None]], axis=0)
    west = jnp.concatenate([grid[:, :1], grid[:, :-1]], axis=1)
    east = jnp.concatenate([grid[:, 1:], grid[:, -1:]], axis=1)
    summed = flux_of(north - grid, level) + flux_of(south - grid, level)
    summed = summed + flux_of(west - grid, level) + flux_of(east - grid, level)
    return grid + diffusion * summed


def per_device(observed, valid_mask, pix_factor, col_factor):
    pix_count = lax.axis_size("pix")
    col_count = lax.axis_size("col")
    pixels, columns = observed.shape
    dates = valid_mask.shape[1]
    weight = jnp.broadcast_to(
        valid_mask.astype(jnp.float32)[:, :, None], (pixels, dates, BANDS)
    ).reshape(pixels, columns)
    total = float(pixels * columns * pix_count * col_count)
    pix_fac = pix_factor
    col_fac = col_factor
    low_rank = jnp.dot(pix_fac, col_fac.T, precision=highest)
    for iteration in range(ITERS):
        residual = observed - low_rank
        level = level_of(residual, weight, total)
        sparse = weight * soft_cut(residual, level)
        misfit = weight * (sparse - residual)
        pix_grad = lax.psum(jnp.dot(misfit, col_fac, precision=highest), "col")
        change = jnp.dot(pix_grad, col_fac.T, precision=highest)
        norm_local = jnp.sum(pix_grad * pix_grad)
        curve_local = jnp.sum(weight * change * change)
        top_sum = lax.psum(norm_local, "pix")
        bottom_sum = lax.psum(curve_local, ("pix", "col"))
        step_pix = top_sum / bottom_sum
        pix_fac = pix_fac - step_pix * pix_grad
        low_rank = low_rank - step_pix * change
        misfit = weight * (sparse - (observed - low_rank))
        local_grad = lax.dot_general(
            misfit,
            pix_fac,
            (((0,), (0,)), ((), ())),
            precision=highest,
            preferred_element_type=jnp.float32,
        )
        col_grad = lax.psum(local_grad, "pix")
        shifted = jnp.dot(pix_fac, col_grad.T, precision=highest)
        norm_local = jnp.sum(col_grad * col_grad)
        curve_local = jnp.sum(weight * shifted * shifted)
        top_sum = lax.psum(norm_local, "col")
        bottom_sum = lax.psum(curve_local, ("pix", "col"))
        step_col = top_sum / bottom_sum
        col_fac = col_fac - step_col * col_grad
        low_rank = low_rank - step_col * shifted
    residual = observed - low_rank
    level = level_of(residual, weight, total)
    layer = weight * soft_cut(residual, level)
    strip_index = lax.axis_index("pix")
    grid = layer.reshape(pixels // WIDTH, WIDTH, columns)
    for sweep_index in range(PASSES):
        grid = smooth_pass(grid, level, strip_index, pix_count)
    return (pix_fac, col_fac, grid.reshape(pixels, columns))


def solution(mesh):
    in_specs = (P("pix", "col"), P("pix", "col"), P("pix", None), P("col", None))
    out_specs = (P("pix", None), P("col", None), P("pix", "col"))
    return jax.shard_map(
        per_device, mesh=mesh, in_specs=in_specs, out_specs=out_specs, check_vma=False
    )
```

profile of v0, /device:TPU:32, one launch (start us, length us, event | category | flops | bytes accessed | tf_op | source)
XLA Modules:
  0.0 2382.3 jit_solution(10405248718728174888)
XLA Ops:
  11.8 7.0 fusion
  18.7 65.8 %psum.105 = f32[]{:T(128)} all-reduce(f32[]{:T(128)} %get-tuple-element.8), channel_id=1, replica_groups=mesh['pix'=64,'col'=2] {'pix','col'}, use_global_device_ids=true, to_apply=%region_1.0 | all-reduce | flops 1 | bytes 8 | tf_op jit(solution)/shard_map/psum | solution.py:30
  85.2 5.7 fusion.20
  91.0 28.1 %all-reduce.5.cloned.1.call-done = f32[256,256]{1,0:T(8,128)} async-done(((f32[256,256]{1,0:T(8,128)}), f32[256,256]{1,0:T(8,128)}) %all-reduce.5.cloned.1.call-update) | async-done | bytes 262160 | tf_op jit(solution)/shard_map/psum | solution.py:69
  120.7 156.7 %psum.107 = f32[]{:T(128)} all-reduce(f32[]{:T(128)} %multiply_reduce_fusion.3), channel_id=1, replica_groups=mesh['pix'=64,'col'=2] {'pix'}, use_global_device_ids=true, to_apply=%region_4.0 | all-reduce | flops 1 | bytes 8 | tf_op jit(solution)/shard_map/psum | solution.py:73
  277.5 5.6 fusion.1
  283.1 72.4 %psum.108 = f32[]{:T(128)} all-reduce(f32[]{:T(128)} %get-tuple-element.19), channel_id=1, replica_groups=mesh['pix'=64,'col'=2] {'pix','col'}, use_global_device_ids=true, to_apply=%region_6.0 | all-reduce | flops 1 | bytes 8 | tf_op jit(solution)/shard_map/psum | solution.py:74
  356.8 9.0 fusion.16
  365.9 638.4 %all-reduce.7.cloned.1.call-done = f32[2048,256]{1,0:T(8,128)} async-done(((f32[2048,256]{1,0:T(8,128)}), f32[2048,256]{1,0:T(8,128)}) %all-reduce.7.cloned.1.call-update) | async-done | bytes 2097168 | tf_op jit(solution)/shard_map/psum | solution.py:86
  1007.0 5.5 psum.110
  1012.5 5.5 fusion.2
  1018.0 68.9 %psum.111 = f32[]{:T(128)} all-reduce(f32[]{:T(128)} %get-tuple-element.21), channel_id=1, replica_groups=mesh['pix'=64,'col'=2] {'pix','col'}, use_global_device_ids=true, to_apply=%region_11.0 | all-reduce | flops 1 | bytes 8 | tf_op jit(solution)/shard_map/psum | solution.py:91
  1088.2 7.4 fusion.3
  1095.6 64.8 %psum.112 = f32[]{:T(128)} all-reduce(f32[]{:T(128)} %get-tuple-element.5), channel_id=1, replica_groups=mesh['pix'=64,'col'=2] {'pix','col'}, use_global_device_ids=true, to_apply=%region_13.0 | all-reduce | flops 1 | bytes 8 | tf_op jit(solution)/shard_map/psum | solution.py:30
  1168.7 27.3 %all-reduce.9.cloned.1.call-done = f32[256,256]{1,0:T(8,128)} async-done(((f32[256,256]{1,0:T(8,128)}), f32[256,256]{1,0:T(8,128)}) %all-reduce.9.cloned.1.call-update) | async-done | bytes 262160 | tf_op jit(solution)/shard_map/psum | solution.py:69
  1197.6 156.7 %psum.114 = f32[]{:T(128)} all-reduce(f32[]{:T(128)} %multiply_reduce_fusion.2), channel_id=1, replica_groups=mesh['pix'=64,'col'=2] {'pix'}, use_global_device_ids=true, to_apply=%region_16.0 | all-reduce | flops 1 | bytes 8 | tf_op jit(solution)/shard_map/psum | solution.py:73
  1354.3 5.6 fusion.4
  1359.9 72.4 %psum.115 = f32[]{:T(128)} all-reduce(f32[]{:T(128)} %get-tuple-element.23), channel_id=1, replica_groups=mesh['pix'=64,'col'=2] {'pix','col'}, use_global_device_ids=true, to_apply=%region_18.0 | all-reduce | flops 1 | bytes 8 | tf_op jit(solution)/shard_map/psum | solution.py:74
  1433.8 9.1 fusion.7
  1442.9 638.5 %all-reduce.11.cloned.1.call-done = f32[2048,256]{1,0:T(8,128)} async-done(((f32[2048,256]{1,0:T(8,128)}), f32[2048,256]{1,0:T(8,128)}) %all-reduce.11.cloned.1.call-update) | async-done | bytes 2097168 | tf_op jit(solution)/shard_map/psum | solution.py:86
  2084.1 5.5 psum.117
  2089.7 5.5 fusion.5
  2095.2 69.0 %psum.118 = f32[]{:T(128)} all-reduce(f32[]{:T(128)} %get-tuple-element.25), channel_id=1, replica_groups=mesh['pix'=64,'col'=2] {'pix','col'}, use_global_device_ids=true, to_apply=%region_23.0 | all-reduce | flops 1 | bytes 8 | tf_op jit(solution)/shard_map/psum | solution.py:91
  2165.4 6.5 fusion.6
  2171.9 64.7 %psum.119 = f32[]{:T(128)} all-reduce(f32[]{:T(128)} %get-tuple-element.3), channel_id=1, replica_groups=mesh['pix'=64,'col'=2] {'pix','col'}, use_global_device_ids=true, to_apply=%region_25.0 | all-reduce | flops 1 | bytes 8 | tf_op jit(solution)/shard_map/psum | solution.py:30
  2237.3 3.7 multiply_multiply_fusion.7
  2241.0 3.5 collective-permute-start.1
  2249.9 38.5 %collective-permute-done.1 = f32[256,2048]{1,0:T(8,128)S(1)} collective-permute-done((f32[256,2048]{1,0:T(8,128)}, f32[256,2048]{1,0:T(8,128)S(1)}, u32[]{:S(2)}, u32[]{:S(2)}) %collective-permute-start.1) | collective-permute-done | bytes 2097184 | tf_op jit(solution)/shard_map/ppermute | solution.py:18
  2288.5 4.2 collective-permute-done
  2292.7 4.4 multiply_add_fusion.1
  2304.3 39.8 %collective-permute-done.3 = f32[256,2048]{1,0:T(8,128)S(1)} collective-permute-done((f32[256,2048]{1,0:T(8,128)S(1)}, f32[256,2048]{1,0:T(8,128)S(1)}, u32[]{:S(2)}, u32[]{:S(2)}) %collective-permute-start.3) | collective-permute-done | bytes 2097184 | tf_op jit(solution)/shard_map/ppermute | solution.py:18
  2344.1 27.9 %collective-permute-done.2 = f32[256,2048]{1,0:T(8,128)S(1)} collective-permute-done((f32[256,2048]{1,0:T(8,128)S(1)}, f32[256,2048]{1,0:T(8,128)S(1)}, u32[]{:S(2)}, u32[]{:S(2)}) %collective-permute-start.2) | collective-permute-done | bytes 2097184 | tf_op jit(solution)/shard_map/ppermute | solution.py:18
  (47 shorter events, 36.9 us)
Async XLA Ops:
  7.2 111.9 %all-reduce.5.cloned.1.call-start = ((), (), s32[]{:S(2)}) async-start(), calls=%async_computation | async-start | bytes 524288 | tf_op jit(solution)/shard_map/psum | solution.py:69
  9.8 2.0 copy-start.8
  91.0 913.3 %all-reduce.7.cloned.1.call-start = ((), (), s32[]{:S(2)}) async-start(), calls=%async_computation.1 | async-start | bytes 4194304 | tf_op jit(solution)/shard_map/psum | solution.py:86
  277.5 79.3 %copy-start.6 = (f32[256,256]{1,0:T(8,128)S(1)}, f32[256,256]{1,0:T(8,128)}, u32[]{:S(2)}) copy-start(f32[256,256]{1,0:T(8,128)} %all-reduce.5.cloned.1.call-done) | copy-start | bytes 786436
  365.8 830.2 %all-reduce.9.cloned.1.call-start = ((), (), s32[]{:S(2)}) async-start(), calls=%async_computation.2 | async-start | bytes 524288 | tf_op jit(solution)/shard_map/psum | solution.py:69
  1161.1 4.0 copy-start.3
  1163.8 1.4 copy-start
  1168.7 912.7 %all-reduce.11.cloned.1.call-start = ((), (), s32[]{:S(2)}) async-start(), calls=%async_computation.3 | async-start | bytes 4194304 | tf_op jit(solution)/shard_map/psum | solution.py:86
  1354.3 79.4 %copy-start.5 = (f32[256,256]{1,0:T(8,128)S(1)}, f32[256,256]{1,0:T(8,128)}, u32[]{:S(2)}) copy-start(f32[256,256]{1,0:T(8,128)} %all-reduce.9.cloned.1.call-done) | copy-start | bytes 786436
  1433.8 655.9 %copy-start.4 = (f32[256,256]{1,0:T(8,128)}, f32[256,256]{1,0:T(8,128)S(1)}, u32[]{:S(2)}) copy-start(f32[256,256]{1,0:T(8,128)S(1)} %multiply_subtract_fusion.7) | copy-start | bytes 786436
  2241.0 47.5 %collective-permute-start.1 = (f32[256,2048]{1,0:T(8,128)}, f32[256,2048]{1,0:T(8,128)S(1)}, u32[]{:S(2)}, u32[]{:S(2)}) collective-permute-start(f32[256,2048]{1,0:T(8,128)} %multiply_multiply_fusion.7), channel_id=1, source_target_pairs={{2,0},{4,2},{6,4},{8,6},{10,8},{12,10},{14,12},{16,14},{18,16},{20... | collective-permute-start | bytes 6291464 | tf_op jit(solution)/shard_map/ppermute | solution.py:18
  2244.6 48.2 %collective-permute-start = (f32[256,2048]{1,0:T(8,128)}, f32[256,2048]{1,0:T(8,128)}, u32[]{:S(2)}, u32[]{:S(2)}) collective-permute-start(f32[256,2048]{1,0:T(8,128)} %multiply_multiply_fusion.7), channel_id=1, source_target_pairs={{0,2},{2,4},{4,6},{6,8},{8,10},{10,12},{12,14},{14,16},{16,18},{18... | collective-permute-start | bytes 6291464 | tf_op jit(solution)/shard_map/ppermute | solution.py:18
  2288.5 4.3 copy-start.7
  2292.7 9.5 copy-start.1
  2292.7 9.5 copy-start.2
  2297.1 47.0 %collective-permute-start.3 = (f32[256,2048]{1,0:T(8,128)S(1)}, f32[256,2048]{1,0:T(8,128)S(1)}, u32[]{:S(2)}, u32[]{:S(2)}) collective-permute-start(f32[256,2048]{1,0:T(8,128)S(1)} %multiply_add_fusion.1), channel_id=1, source_target_pairs={{2,0},{4,2},{6,4},{8,6},{10,8},{12,10},{14,12},{16,14},{18,16},{20... | collective-permute-start | bytes 6291464 | tf_op jit(solution)/shard_map/ppermute | solution.py:18
  2300.3 71.6 %collective-permute-start.2 = (f32[256,2048]{1,0:T(8,128)S(1)}, f32[256,2048]{1,0:T(8,128)S(1)}, u32[]{:S(2)}, u32[]{:S(2)}) collective-permute-start(f32[256,2048]{1,0:T(8,128)S(1)} %multiply_add_fusion.1), channel_id=1, source_target_pairs={{0,2},{2,4},{4,6},{6,8},{8,10},{10,12},{12,14},{14,16},{16,18},{18... | collective-permute-start | bytes 6291464 | tf_op jit(solution)/shard_map/ppermute | solution.py:18
Sparse Core Ops, SparseCore 0:
  91.1 27.9 all-reduce.4
  366.0 638.2 all-reduce.6
  1168.8 27.1 all-reduce.8
  1443.0 638.2 all-reduce.10
where the time goes:
time: 2390 us; the launch traced here: 2380 us
  waiting for transfers between devices  1440 us (60%)
  blocking collectives  803 us (34%)
  matrix products  56.5 us (2%)
  other arithmetic  39.3 us (2%)
    psum x2, waiting for transfers between devices, per_device(): col_grad = lax.psum(local_grad, 'pix')  1280 us
    psum x2, blocking collectives, per_device(): top_sum = lax.psum(norm_local, 'pix')  313 us
    psum x4, blocking collectives, per_device(): bottom_sum = lax.psum(curve_local, ('pix', 'col'))  283 us
    psum x3, blocking collectives, level_of(): spread = lax.psum(jnp.sum(weight * residual * residual), ('pix', 'col'))  195 us
    ppermute x4, waiting for transfers between devices, passed_along(): return lax.ppermute(block, axis, route)  110 us
    psum x2, waiting for transfers between devices, per_device(): pix_grad = lax.psum(jnp.dot(misfit, col_fac, precision=highest), 'col')  55.3 us
  transfers between devices with their start and end apart: 8, of which 8 were waited for; matrix products, arithmetic and copies ran while one was open for 0% of the time, Pallas kernels for 0%

commit v1 on v0

--- a/solution.py
+++ b/solution.py
@@ -71,7 +71,7 @@
         norm_local = jnp.sum(pix_grad * pix_grad)
         curve_local = jnp.sum(weight * change * change)
         top_sum = lax.psum(norm_local, "pix")
-        bottom_sum = lax.psum(curve_local, ("pix", "col"))
+        bottom_sum = lax.psum(lax.psum(curve_local, "col"), "pix")
         step_pix = top_sum / bottom_sum
         pix_fac = pix_fac - step_pix * pix_grad
         low_rank = low_rank - step_pix * change

time: 2390 us -> 2270 us (0.950)
  blocking collectives: 803 us -> 667 us
    psum x4 -> x2, blocking collectives: 283 us -> 138 us  [per_device(): bottom_sum = lax.psum(curve_local, ('pix', 'col'))]
where the time goes in v1:
time: 2270 us; the launch traced here: 2260 us
  waiting for transfers between devices  1460 us (64%)
  blocking collectives  667 us (29%)
  matrix products  56.5 us (2%)
  other arithmetic  39.3 us (2%)
    psum x2, waiting for transfers between devices, per_device(): col_grad = lax.psum(local_grad, 'pix')  1290 us
    psum x2, blocking collectives, per_device(): top_sum = lax.psum(norm_local, 'pix')  312 us
    psum x3, blocking collectives, level_of(): spread = lax.psum(jnp.sum(weight * residual * residual), ('pix', 'col'))  195 us
    psum x2, blocking collectives, per_device(): bottom_sum = lax.psum(curve_local, ('pix', 'col'))  138 us
    ppermute x4, waiting for transfers between devices, passed_along(): return lax.ppermute(block, axis, route)  110 us
    psum x2, waiting for transfers between devices, per_device(): pix_grad = lax.psum(jnp.dot(misfit, col_fac, precision=highest), 'col')  55.3 us
  transfers between devices with their start and end apart: 8, of which 8 were waited for; matrix products, arithmetic and copies ran while one was open for 0% of the time, Pallas kernels for 0%

profile of v1, /device:TPU:32, one launch (start us, length us, event | category | flops | bytes accessed | tf_op | source)
XLA Modules:
  0.0 2260.7 jit_solution(12492873241208168827)
XLA Ops:
  11.8 7.0 fusion
  18.7 65.8 %psum.119 = f32[]{:T(128)} all-reduce(f32[]{:T(128)} %get-tuple-element.12), channel_id=1, replica_groups=mesh['pix'=64,'col'=2] {'pix','col'}, use_global_device_ids=true, to_apply=%region_1.0 | all-reduce | flops 1 | bytes 8 | tf_op jit(solution)/shard_map/psum | solution.py:30
  85.2 5.7 fusion.20
  91.0 28.1 %all-reduce.7.cloned.1.call-done = f32[256,256]{1,0:T(8,128)} async-done(((f32[256,256]{1,0:T(8,128)}), f32[256,256]{1,0:T(8,128)}) %all-reduce.7.cloned.1.call-update) | async-done | bytes 262160 | tf_op jit(solution)/shard_map/psum | solution.py:69
  120.7 5.6 fusion.1
  126.4 5.6 psum.122
  131.9 156.1 %all-reduce.1 = (f32[]{:T(128)}, f32[]{:T(128)}) all-reduce(f32[]{:T(128)} %multiply_reduce_fusion.3, f32[]{:T(128)} %psum.122), channel_id=1, replica_groups=mesh['pix'=64,'col'=2] {'pix'}, use_global_device_ids=true, to_apply=%region_4.0 | all-reduce | flops 2 | bytes 16 | tf_op jit(solution)/shard_map/psum | solution.py:73
  289.3 9.0 fusion.16
  298.4 645.4 %all-reduce.9.cloned.1.call-done = f32[2048,256]{1,0:T(8,128)} async-done(((f32[2048,256]{1,0:T(8,128)}), f32[2048,256]{1,0:T(8,128)}) %all-reduce.9.cloned.1.call-update) | async-done | bytes 2097168 | tf_op jit(solution)/shard_map/psum | solution.py:86
  946.6 5.5 psum.125
  952.1 5.5 fusion.2
  957.6 68.9 %psum.126 = f32[]{:T(128)} all-reduce(f32[]{:T(128)} %get-tuple-element.25), channel_id=1, replica_groups=mesh['pix'=64,'col'=2] {'pix','col'}, use_global_device_ids=true, to_apply=%region_12.0 | all-reduce | flops 1 | bytes 8 | tf_op jit(solution)/shard_map/psum | solution.py:91
  1027.8 7.4 fusion.3
  1035.3 64.7 %psum.127 = f32[]{:T(128)} all-reduce(f32[]{:T(128)} %get-tuple-element.9), channel_id=1, replica_groups=mesh['pix'=64,'col'=2] {'pix','col'}, use_global_device_ids=true, to_apply=%region_14.0 | all-reduce | flops 1 | bytes 8 | tf_op jit(solution)/shard_map/psum | solution.py:30
  1108.3 27.3 %all-reduce.11.cloned.1.call-done = f32[256,256]{1,0:T(8,128)} async-done(((f32[256,256]{1,0:T(8,128)}), f32[256,256]{1,0:T(8,128)}) %all-reduce.11.cloned.1.call-update) | async-done | bytes 262160 | tf_op jit(solution)/shard_map/psum | solution.py:69
  1137.2 5.6 fusion.4
  1142.8 5.6 psum.130
  1148.4 155.7 %all-reduce = (f32[]{:T(128)}, f32[]{:T(128)}) all-reduce(f32[]{:T(128)} %multiply_reduce_fusion.2, f32[]{:T(128)} %psum.130), channel_id=1, replica_groups=mesh['pix'=64,'col'=2] {'pix'}, use_global_device_ids=true, to_apply=%region_17.0 | all-reduce | flops 2 | bytes 16 | tf_op jit(solution)/shard_map/psum | solution.py:73
  1305.5 9.1 fusion.7
  1314.6 645.5 %all-reduce.13.cloned.1.call-done = f32[2048,256]{1,0:T(8,128)} async-done(((f32[2048,256]{1,0:T(8,128)}), f32[2048,256]{1,0:T(8,128)}) %all-reduce.13.cloned.1.call-update) | async-done | bytes 2097168 | tf_op jit(solution)/shard_map/psum | solution.py:86
  1962.9 5.8 psum.133
  1968.6 5.5 fusion.5
  1974.1 69.0 %psum.134 = f32[]{:T(128)} all-reduce(f32[]{:T(128)} %get-tuple-element.29), channel_id=1, replica_groups=mesh['pix'=64,'col'=2] {'pix','col'}, use_global_device_ids=true, to_apply=%region_25.0 | all-reduce | flops 1 | bytes 8 | tf_op jit(solution)/shard_map/psum | solution.py:91
  2044.4 6.5 fusion.6
  2050.9 64.4 %psum.135 = f32[]{:T(128)} all-reduce(f32[]{:T(128)} %get-tuple-element.7), channel_id=1, replica_groups=mesh['pix'=64,'col'=2] {'pix','col'}, use_global_device_ids=true, to_apply=%region_27.0 | all-reduce | flops 1 | bytes 8 | tf_op jit(solution)/shard_map/psum | solution.py:30
  2116.0 3.7 multiply_multiply_fusion.7
  2119.7 3.5 collective-permute-start.1
  2128.6 38.5 %collective-permute-done.1 = f32[256,2048]{1,0:T(8,128)S(1)} collective-permute-done((f32[256,2048]{1,0:T(8,128)}, f32[256,2048]{1,0:T(8,128)S(1)}, u32[]{:S(2)}, u32[]{:S(2)}) %collective-permute-start.1) | collective-permute-done | bytes 2097184 | tf_op jit(solution)/shard_map/ppermute | solution.py:18
  2167.1 4.2 collective-permute-done
  2171.4 4.4 multiply_add_fusion.1
  2183.0 39.8 %collective-permute-done.3 = f32[256,2048]{1,0:T(8,128)S(1)} collective-permute-done((f32[256,2048]{1,0:T(8,128)S(1)}, f32[256,2048]{1,0:T(8,128)S(1)}, u32[]{:S(2)}, u32[]{:S(2)}) %collective-permute-start.3) | collective-permute-done | bytes 2097184 | tf_op jit(solution)/shard_map/ppermute | solution.py:18
  2222.7 27.9 %collective-permute-done.2 = f32[256,2048]{1,0:T(8,128)S(1)} collective-permute-done((f32[256,2048]{1,0:T(8,128)S(1)}, f32[256,2048]{1,0:T(8,128)S(1)}, u32[]{:S(2)}, u32[]{:S(2)}) %collective-permute-start.2) | collective-permute-done | bytes 2097184 | tf_op jit(solution)/shard_map/ppermute | solution.py:18
  (47 shorter events, 36.9 us)
Async XLA Ops:
  7.2 111.9 %all-reduce.7.cloned.1.call-start = ((), (), s32[]{:S(2)}) async-start(), calls=%async_computation | async-start | bytes 524288 | tf_op jit(solution)/shard_map/psum | solution.py:69
  9.8 2.0 copy-start.8
  91.0 852.9 %all-reduce.9.cloned.1.call-start = ((), (), s32[]{:S(2)}) async-start(), calls=%async_computation.1 | async-start | bytes 4194304 | tf_op jit(solution)/shard_map/psum | solution.py:86
  120.7 168.5 %copy-start.6 = (f32[256,256]{1,0:T(8,128)S(1)}, f32[256,256]{1,0:T(8,128)}, u32[]{:S(2)}) copy-start(f32[256,256]{1,0:T(8,128)} %all-reduce.7.cloned.1.call-done) | copy-start | bytes 786436
  298.4 837.2 %all-reduce.11.cloned.1.call-start = ((), (), s32[]{:S(2)}) async-start(), calls=%async_computation.2 | async-start | bytes 524288 | tf_op jit(solution)/shard_map/psum | solution.py:69
  1100.7 4.0 copy-start.3
  1103.4 1.4 copy-start
  1108.3 851.9 %all-reduce.13.cloned.1.call-start = ((), (), s32[]{:S(2)}) async-start(), calls=%async_computation.3 | async-start | bytes 4194304 | tf_op jit(solution)/shard_map/psum | solution.py:86
  1137.2 168.2 %copy-start.5 = (f32[256,256]{1,0:T(8,128)S(1)}, f32[256,256]{1,0:T(8,128)}, u32[]{:S(2)}) copy-start(f32[256,256]{1,0:T(8,128)} %all-reduce.11.cloned.1.call-done) | copy-start | bytes 786436
  1305.5 663.1 %copy-start.4 = (f32[256,256]{1,0:T(8,128)}, f32[256,256]{1,0:T(8,128)S(1)}, u32[]{:S(2)}) copy-start(f32[256,256]{1,0:T(8,128)S(1)} %multiply_subtract_fusion.7) | copy-start | bytes 786436
  2119.7 47.5 %collective-permute-start.1 = (f32[256,2048]{1,0:T(8,128)}, f32[256,2048]{1,0:T(8,128)S(1)}, u32[]{:S(2)}, u32[]{:S(2)}) collective-permute-start(f32[256,2048]{1,0:T(8,128)} %multiply_multiply_fusion.7), channel_id=1, source_target_pairs={{2,0},{4,2},{6,4},{8,6},{10,8},{12,10},{14,12},{16,14},{18,16},{20... | collective-permute-start | bytes 6291464 | tf_op jit(solution)/shard_map/ppermute | solution.py:18
  2123.2 48.2 %collective-permute-start = (f32[256,2048]{1,0:T(8,128)}, f32[256,2048]{1,0:T(8,128)}, u32[]{:S(2)}, u32[]{:S(2)}) collective-permute-start(f32[256,2048]{1,0:T(8,128)} %multiply_multiply_fusion.7), channel_id=1, source_target_pairs={{0,2},{2,4},{4,6},{6,8},{8,10},{10,12},{12,14},{14,16},{16,18},{18... | collective-permute-start | bytes 6291464 | tf_op jit(solution)/shard_map/ppermute | solution.py:18
  2167.1 4.3 copy-start.7
  2171.4 9.5 copy-start.1
  2171.4 9.5 copy-start.2
  2175.8 47.0 %collective-permute-start.3 = (f32[256,2048]{1,0:T(8,128)S(1)}, f32[256,2048]{1,0:T(8,128)S(1)}, u32[]{:S(2)}, u32[]{:S(2)}) collective-permute-start(f32[256,2048]{1,0:T(8,128)S(1)} %multiply_add_fusion.1), channel_id=1, source_target_pairs={{2,0},{4,2},{6,4},{8,6},{10,8},{12,10},{14,12},{16,14},{18,16},{20... | collective-permute-start | bytes 6291464 | tf_op jit(solution)/shard_map/ppermute | solution.py:18
  2179.0 71.6 %collective-permute-start.2 = (f32[256,2048]{1,0:T(8,128)S(1)}, f32[256,2048]{1,0:T(8,128)S(1)}, u32[]{:S(2)}, u32[]{:S(2)}) collective-permute-start(f32[256,2048]{1,0:T(8,128)S(1)} %multiply_add_fusion.1), channel_id=1, source_target_pairs={{0,2},{2,4},{4,6},{6,8},{8,10},{10,12},{12,14},{14,16},{16,18},{18... | collective-permute-start | bytes 6291464 | tf_op jit(solution)/shard_map/ppermute | solution.py:18
Sparse Core Ops, SparseCore 0:
  91.1 27.9 all-reduce.6
  298.5 645.3 all-reduce.8
  1108.4 27.1 all-reduce.10
  1314.7 645.3 all-reduce.12
